TPU v7x, 32 devices: a whole 2x2x4 slice. The times are simulated.
32 devices in a mesh: layer: 4 (over x, core), grid: 8 (over z, y).
Axes of the slice: x: 2, y: 2, z: 4, core: 2. Of those that a mesh axis runs over, the one named last changes fastest.
Arguments:
- band_blocks: bfloat16 [80, 9, 128, 128], P('grid'), may hold values from -7 to 7, as said below
- retained: int32 [80, 9], P('grid'), may hold values from 0 to 1, as said below
Outputs:
- purified: bfloat16 [80, 9, 128, 128], P('grid', None, 'layer')
Inputs may be any that keep to these rules, and one draw needn't show every extreme that they name: `band_blocks`: the matrix is symmetric: block slot w of block row i equals the transpose of block slot 8 - w of block row (i + w - 4) mod 80. retained[i, w] = 1 exactly when retained[(i + w - 4) mod 80, 8 - w] = 1; the middle slot w = 4 is 1 in every block row.
All inputs are finite; a program needn't handle non-finite values.
Results may differ from a plain program's by a relative error of at most 0.005.
Values may be sent and summed in bfloat16 or wider, within the bound.
A program may use at most 64 MiB of HBM per device.

v0:
```python
import jax
import jax.numpy as jnp
from jax import lax
from jax.sharding import PartitionSpec as P

STEPS = 2


def extended(block, sides, width):
    for axis, dim in sides:
        count = lax.axis_size(axis)
        forward = [(i, i + 1) for i in range(count - 1)]
        forward.append((count - 1, 0))
        backward = [(target, source) for source, target in forward]
        low = lax.ppermute(
            lax.slice_in_dim(block, block.shape[dim] - width, None, axis=dim), axis, forward
        )
        high = lax.ppermute(lax.slice_in_dim(block, 0, width, axis=dim), axis, backward)
        block = jnp.concatenate([low, block, high], axis=dim)
    return block


def strip_product(left_rows, halo_rows, reach):
    row_count = left_rows.shape[0]
    band_width = left_rows.shape[1]
    padded = jnp.pad(halo_rows, ((0, 0), (reach, reach), (0, 0), (0, 0)))
    running = jnp.zeros(
        (row_count, band_width, left_rows.shape[2], halo_rows.shape[3]), jnp.float32
    )
    for offset in range(band_width):
        source = padded[
            offset : offset + row_count, 2 * reach - offset : 2 * reach - offset + band_width
        ]
        running = running + jnp.einsum(
            "rab,rwbc->rwac", left_rows[:, offset], source, preferred_element_type=jnp.float32
        )
    return running


def per_device(band_blocks, retained):
    layer_count = lax.axis_size("layer")
    share = lax.axis_index("layer")
    band_width = band_blocks.shape[1]
    block_width = band_blocks.shape[2]
    reach = (band_width - 1) // 2
    piece = block_width // layer_count
    kept = (retained != 0)[:, :, None, None]
    whole_rows = jnp.where(kept, band_blocks, jnp.zeros_like(band_blocks))
    quarter = lax.dynamic_slice_in_dim(whole_rows, share * piece, piece, 2)
    for repeat in range(STEPS):
        halo_part = extended(quarter, (("grid", 0),), reach)
        halo_rows = lax.all_gather(halo_part, "layer", axis=2, tiled=True)
        square = jnp.where(kept, strip_product(quarter, halo_rows, reach), 0.0).astype(jnp.bfloat16)
        cube = jnp.where(kept, strip_product(square, halo_rows, reach), 0.0)
        quarter = (
            (3.0 * quarter.astype(jnp.float32) - cube / (4.0 * band_width * block_width)) * 0.5
        ).astype(jnp.bfloat16)
    return quarter


def solution(mesh):
    return jax.shard_map(
        per_device,
        mesh=mesh,
        in_specs=(P("grid", None, None, None), P("grid", None)),
        out_specs=P("grid", None, "layer", None),
        check_vma=False,
    )
```

profile of v0, /device:TPU:0, one launch (start us, length us, event | category | flops | bytes accessed | tf_op | source)
XLA Modules:
  0.0 161.0 jit_solution(15024510150904314228)
XLA Ops:
  6.5 0.9 broadcast_compare_fusion
  7.4 0.1 copy.3
  7.5 0.9 copy-done
  8.4 0.2 copy_select_fusion
  8.6 0.0 copy-start.7
  8.7 3.0 %collective-permute-start = (bf16[4,9,32,128]{3,2,0,1:T(8,128)(2,1)S(1)}, bf16[4,9,32,128]{3,2,0,1:T(8,128)(2,1)S(1)}, u32[]{:S(2)}, u32[]{:S(2)}) collective-permute-start(bf16[4,9,32,128]{3,2,0,1:T(8,128)(2,1)S(1)} %get-tuple-element.7), channel_id=1, source_target_pairs={{0,1},{1,2},{2,3},{3,4},{4,5},{5,6},{6,7},{7,0},{8,9},{9,10},{10,1... | collective-permute-start | bytes 884744 | tf_op jit(solution)/shard_map/ppermute | solution.py:15
  11.7 3.1 %collective-permute-start.1 = (bf16[4,9,32,128]{3,2,0,1:T(8,128)(2,1)S(1)}, bf16[4,9,32,128]{3,2,0,1:T(8,128)(2,1)S(1)}, u32[]{:S(2)}, u32[]{:S(2)}) collective-permute-start(bf16[4,9,32,128]{3,2,0,1:T(8,128)(2,1)S(1)} %get-tuple-element.8), channel_id=1, source_target_pairs={{1,0},{2,1},{3,2},{4,3},{5,4},{6,5},{7,6},{0,7},{9,8},{10,9},{11,1... | collective-permute-start | bytes 884744 | tf_op jit(solution)/shard_map/ppermute | solution.py:18
  14.8 9.5 %collective-permute-done = bf16[4,9,32,128]{3,2,0,1:T(8,128)(2,1)S(1)} collective-permute-done((bf16[4,9,32,128]{3,2,0,1:T(8,128)(2,1)S(1)}, bf16[4,9,32,128]{3,2,0,1:T(8,128)(2,1)S(1)}, u32[]{:S(2)}, u32[]{:S(2)}) %collective-permute-start) | collective-permute-done | bytes 294944 | tf_op jit(solution)/shard_map/ppermute | solution.py:15
  24.3 2.2 %collective-permute-done.1 = bf16[4,9,32,128]{3,2,0,1:T(8,128)(2,1)S(1)} collective-permute-done((bf16[4,9,32,128]{3,2,0,1:T(8,128)(2,1)S(1)}, bf16[4,9,32,128]{3,2,0,1:T(8,128)(2,1)S(1)}, u32[]{:S(2)}, u32[]{:S(2)}) %collective-permute-start.1) | collective-permute-done | bytes 294944 | tf_op jit(solution)/shard_map/ppermute | solution.py:18
  26.5 1.3 pad_maximum_fusion
  27.8 0.0 all-gather.3.cloned.1.call-update
  27.8 0.0 all-gather.5.cloned.1.call-start
  27.8 40.9 %all-gather.3.cloned.1.call-done = bf16[18,9,128,128]{3,2,0,1:T(8,128)(2,1)} async-done(((bf16[18,9,32,128]{3,2,0,1:T(8,128)(2,1)}), bf16[18,9,128,128]{3,2,0,1:T(8,128)(2,1)}) %all-gather.3.cloned.1.call-update) | async-done | bytes 5308432 | tf_op jit(solution)/shard_map/all_gather | solution.py:52
  68.7 2.2 %fusion.24 = f32[10,9,128,32]{2,3,0,1:T(8,128)S(1)} fusion(bf16[18,9,128,128]{3,2,0,1:T(8,128)(2,1)} %all-gather.3.cloned.1.call-done, bf16[10,9,32,128]{3,2,0,1:T(8,128)(2,1)} %copy-done.7), kind=kOutput, calls=%fused_computation.44 | convolution fusion | flops 94371840 | bytes 6864896 | tf_op jit(solution)/shard_map/rab,rwbc->rwac/dot_general | solution.py:34
  71.0 0.9 copy-done.2
  71.9 0.2 copy-done.8
  72.1 0.5 fusion.22
  72.5 0.6 fusion.20
  73.1 0.6 fusion.18
  73.7 0.5 fusion.16
  74.2 0.5 fusion.14
  74.6 0.5 fusion.12
  75.1 0.6 fusion.4
  75.7 0.9 fusion.40
  76.6 0.5 fusion.25
  77.0 0.5 fusion.23
  77.5 0.6 fusion.21
  78.1 0.6 fusion.6
  78.7 0.6 fusion.19
  79.2 0.5 fusion.17
  79.7 0.5 fusion.15
  80.2 0.5 fusion.13
  80.7 1.1 fusion.11
  81.8 0.0 copy-start.4
  81.9 1.5 collective-permute-start.2
  83.4 3.3 %collective-permute-start.3 = (bf16[4,9,32,128]{3,2,0,1:T(8,128)(2,1)S(1)}, bf16[4,9,32,128]{3,2,0,1:T(8,128)(2,1)S(1)}, u32[]{:S(2)}, u32[]{:S(2)}) collective-permute-start(bf16[4,9,32,128]{3,2,0,1:T(8,128)(2,1)S(1)} %get-tuple-element.6), channel_id=1, source_target_pairs={{1,0},{2,1},{3,2},{4,3},{5,4},{6,5},{7,6},{0,7},{9,8},{10,9},{11,1... | collective-permute-start | bytes 884744 | tf_op jit(solution)/shard_map/ppermute | solution.py:18
  86.7 9.8 %collective-permute-done.2 = bf16[4,9,32,128]{3,2,0,1:T(8,128)(2,1)S(1)} collective-permute-done((bf16[4,9,32,128]{3,2,0,1:T(8,128)(2,1)S(1)}, bf16[4,9,32,128]{3,2,0,1:T(8,128)(2,1)S(1)}, u32[]{:S(2)}, u32[]{:S(2)}) %collective-permute-start.2) | collective-permute-done | bytes 294944 | tf_op jit(solution)/shard_map/ppermute | solution.py:15
  96.4 2.2 %collective-permute-done.3 = bf16[4,9,32,128]{3,2,0,1:T(8,128)(2,1)S(1)} collective-permute-done((bf16[4,9,32,128]{3,2,0,1:T(8,128)(2,1)S(1)}, bf16[4,9,32,128]{3,2,0,1:T(8,128)(2,1)S(1)}, u32[]{:S(2)}, u32[]{:S(2)}) %collective-permute-start.3) | collective-permute-done | bytes 294944 | tf_op jit(solution)/shard_map/ppermute | solution.py:18
  98.6 1.3 pad_maximum_fusion.1
  99.9 0.0 all-gather.5.cloned.1.call-update
  99.9 0.0 copy-start.5
  99.9 39.7 %all-gather.5.cloned.1.call-done = bf16[18,9,128,128]{3,2,0,1:T(8,128)(2,1)} async-done(((bf16[18,9,32,128]{3,2,0,1:T(8,128)(2,1)}), bf16[18,9,128,128]{3,2,0,1:T(8,128)(2,1)}) %all-gather.5.cloned.1.call-update) | async-done | bytes 5308432 | tf_op jit(solution)/shard_map/all_gather | solution.py:52
  139.7 2.2 %fusion.38 = f32[10,9,128,32]{2,3,0,1:T(8,128)S(1)} fusion(bf16[18,9,128,128]{3,2,0,1:T(8,128)(2,1)} %all-gather.5.cloned.1.call-done, bf16[10,9,32,128]{3,2,0,1:T(8,128)(2,1)} %copy-done.4), kind=kOutput, calls=%fused_computation.58 | convolution fusion | flops 94371840 | bytes 6864896 | tf_op jit(solution)/shard_map/rab,rwbc->rwac/dot_general | solution.py:34
  141.9 0.9 copy-done.3
  142.8 0.5 fusion.36
  143.3 0.6 fusion.34
  143.8 0.6 fusion.32
  144.4 0.5 fusion.30
  144.9 0.5 fusion.28
  145.4 0.5 fusion.26
  145.9 0.6 fusion
  146.4 1.0 fusion.41
  147.4 0.5 fusion.39
  147.9 0.5 fusion.37
  148.4 0.6 fusion.35
  149.0 0.6 fusion.2
  149.5 0.6 fusion.33
  150.1 0.5 fusion.31
  150.6 0.5 fusion.29
  151.1 0.0 copy-start.6
  151.1 0.5 fusion.27
  151.6 0.6 copy-done.6
  152.2 1.0 fusion.9
  153.2 0.9 copy.78
  (12 shorter events, 0.1 us)
Async XLA Ops:
  6.5 1.8 %copy-start = (bf16[10,9,128,128]{3,2,1,0:T(8,128)(2,1)S(1)}, bf16[10,9,128,128]{3,2,1,0:T(8,128)(2,1)}, u32[]{:S(2)}) copy-start(bf16[10,9,128,128]{3,2,1,0:T(8,128)(2,1)} %param.2) | copy-start | bytes 8847364
  6.5 62.2 %all-gather.3.cloned.1.call-start = ((), (), s32[]{:S(2)}) async-start(), calls=%async_computation | async-start | bytes 6635520 | tf_op jit(solution)/shard_map/all_gather | solution.py:52
  8.6 17.9 %copy-start.7 = (bf16[10,9,32,128]{3,2,0,1:T(8,128)(2,1)}, bf16[10,9,32,128]{3,2,0,1:T(8,128)(2,1)S(1)}, u32[]{:S(2)}) copy-start(bf16[10,9,32,128]{3,2,0,1:T(8,128)(2,1)S(1)} %copy_select_fusion) | copy-start | bytes 2211844
  8.7 15.6 %collective-permute-start = (bf16[4,9,32,128]{3,2,0,1:T(8,128)(2,1)S(1)}, bf16[4,9,32,128]{3,2,0,1:T(8,128)(2,1)S(1)}, u32[]{:S(2)}, u32[]{:S(2)}) collective-permute-start(bf16[4,9,32,128]{3,2,0,1:T(8,128)(2,1)S(1)} %get-tuple-element.7), channel_id=1, source_target_pairs={{0,1},{1,2},{2,3},{3,4},{4,5},{5,6},{6,7},{7,0},{8,9},{9,10},{10,1... | collective-permute-start | bytes 884744 | tf_op jit(solution)/shard_map/ppermute | solution.py:15
  11.7 14.8 %collective-permute-start.1 = (bf16[4,9,32,128]{3,2,0,1:T(8,128)(2,1)S(1)}, bf16[4,9,32,128]{3,2,0,1:T(8,128)(2,1)S(1)}, u32[]{:S(2)}, u32[]{:S(2)}) collective-permute-start(bf16[4,9,32,128]{3,2,0,1:T(8,128)(2,1)S(1)} %get-tuple-element.8), channel_id=1, source_target_pairs={{1,0},{2,1},{3,2},{4,3},{5,4},{6,5},{7,6},{0,7},{9,8},{10,9},{11,1... | collective-permute-start | bytes 884744 | tf_op jit(solution)/shard_map/ppermute | solution.py:18
  27.8 111.9 %all-gather.5.cloned.1.call-start = ((), (), s32[]{:S(2)}) async-start(), calls=%async_computation.1 | async-start | bytes 6635520 | tf_op jit(solution)/shard_map/all_gather | solution.py:52
  68.7 3.1 %copy-start.2 = (bf16[18,9,128,128]{3,2,0,1:T(8,128)(2,1)S(1)}, bf16[18,9,128,128]{3,2,0,1:T(8,128)(2,1)}, u32[]{:S(2)}) copy-start(bf16[18,9,128,128]{3,2,0,1:T(8,128)(2,1)} %all-gather.3.cloned.1.call-done) | copy-start | bytes 15925252
  68.7 3.3 %copy-start.8 = (bf16[10,9,32,128]{3,2,0,1:T(8,128)(2,1)S(1)}, bf16[10,9,32,128]{3,2,0,1:T(8,128)(2,1)}, u32[]{:S(2)}) copy-start(bf16[10,9,32,128]{3,2,0,1:T(8,128)(2,1)} %copy-done.7) | copy-start | bytes 2211844
  81.8 16.8 %copy-start.4 = (bf16[10,9,32,128]{3,2,0,1:T(8,128)(2,1)}, bf16[10,9,32,128]{3,2,0,1:T(8,128)(2,1)S(1)}, u32[]{:S(2)}) copy-start(bf16[10,9,32,128]{3,2,0,1:T(8,128)(2,1)S(1)} %fusion.11) | copy-start | bytes 2211844
  81.9 14.5 %collective-permute-start.2 = (bf16[4,9,32,128]{3,2,0,1:T(8,128)(2,1)S(1)}, bf16[4,9,32,128]{3,2,0,1:T(8,128)(2,1)S(1)}, u32[]{:S(2)}, u32[]{:S(2)}) collective-permute-start(bf16[4,9,32,128]{3,2,0,1:T(8,128)(2,1)S(1)} %get-tuple-element.5), channel_id=1, source_target_pairs={{0,1},{1,2},{2,3},{3,4},{4,5},{5,6},{6,7},{7,0},{8,9},{9,10},{10,1... | collective-permute-start | bytes 884744 | tf_op jit(solution)/shard_map/ppermute | solution.py:15
  83.4 15.2 %collective-permute-start.3 = (bf16[4,9,32,128]{3,2,0,1:T(8,128)(2,1)S(1)}, bf16[4,9,32,128]{3,2,0,1:T(8,128)(2,1)S(1)}, u32[]{:S(2)}, u32[]{:S(2)}) collective-permute-start(bf16[4,9,32,128]{3,2,0,1:T(8,128)(2,1)S(1)} %get-tuple-element.6), channel_id=1, source_target_pairs={{1,0},{2,1},{3,2},{4,3},{5,4},{6,5},{7,6},{0,7},{9,8},{10,9},{11,1... | collective-permute-start | bytes 884744 | tf_op jit(solution)/shard_map/ppermute | solution.py:18
  99.9 42.0 %copy-start.5 = (bf16[10,9,32,128]{3,2,0,1:T(8,128)(2,1)S(1)}, bf16[10,9,32,128]{3,2,0,1:T(8,128)(2,1)}, u32[]{:S(2)}) copy-start(bf16[10,9,32,128]{3,2,0,1:T(8,128)(2,1)} %copy-done.4) | copy-start | bytes 2211844
  139.7 3.1 %copy-start.3 = (bf16[18,9,128,128]{3,2,0,1:T(8,128)(2,1)S(1)}, bf16[18,9,128,128]{3,2,0,1:T(8,128)(2,1)}, u32[]{:S(2)}) copy-start(bf16[18,9,128,128]{3,2,0,1:T(8,128)(2,1)} %all-gather.5.cloned.1.call-done) | copy-start | bytes 15925252
  151.1 1.1 copy-start.6
  152.2 1.9 %copy-start.1 = (bf16[10,9,128,128]{3,2,1,0:T(8,128)(2,1)S(1)}, bf16[10,9,128,128]{3,2,1,0:T(8,128)(2,1)}, u32[]{:S(2)}) copy-start(bf16[10,9,128,128]{3,2,1,0:T(8,128)(2,1)} %param.2) | copy-start | bytes 8847364
Sparse Core Ops, SparseCore 0:
  27.9 40.7 all-gather.2
  100.0 39.5 all-gather.4
where the time goes:
time: 161 us
  waiting for transfers between devices  104 us (65%)
  matrix products  23.9 us (15%)
  between operations  13.6 us (8%)
  starting transfers between devices  11 us (7%)
  local copies, waits for them, and re-layouts  4.62 us (3%)
  other arithmetic  3.59 us (2%)
    all_gather x2, waiting for transfers between devices, per_device(): halo_rows = lax.all_gather(halo_part, 'layer', axis=2, tiled=True)  80.6 us
    dot_general x36, matrix products, strip_product(): jnp.einsum('rab,rwbc->rwac', left_rows[:, offset], source, preferred_elem...  23.9 us
    ppermute x2, waiting for transfers between devices, extended(): lax.ppermute(lax.slice_in_dim(block, block.shape[dim] - width, None, axis...  19.2 us
    ppermute x2, starting transfers between devices, extended(): lax.ppermute(lax.slice_in_dim(block, 0, width, axis=dim), axis, backward)  6.36 us
    ppermute x2, starting transfers between devices, extended(): lax.ppermute(lax.slice_in_dim(block, block.shape[dim] - width, None, axis...  4.57 us
    ppermute x2, waiting for transfers between devices, extended(): lax.ppermute(lax.slice_in_dim(block, 0, width, axis=dim), axis, backward)  4.4 us
    unnamed x18, local copies, waits for them, and re-layouts  3.52 us
  transfers between devices with their start and end apart: 6, of which 6 were waited for; matrix products, arithmetic and copies ran while one was open for 0% of the time, Pallas kernels for 0%

commit v1 on v0

--- a/solution.py
+++ b/solution.py
@@ -4,6 +4,24 @@
 from jax.sharding import PartitionSpec as P
 
 STEPS = 2
+
+
+def gather_around(shard, axis, dim):
+    ways, here, step = (lax.axis_size(axis), lax.axis_index(axis), shard.shape[dim])
+    dims = [n * ways if d == dim else n for d, n in enumerate(shard.shape)]
+    full = lax.dynamic_update_slice_in_dim(
+        jnp.zeros(dims, shard.dtype), shard, here * step, axis=dim
+    )
+    going_up = going_down = shard
+    for far in range(1, ways // 2 + 1):
+        going_up = lax.ppermute(going_up, axis, [(d, (d + 1) % ways) for d in range(ways)])
+        full = lax.dynamic_update_slice_in_dim(full, going_up, (here - far) % ways * step, axis=dim)
+        if 2 * far < ways:
+            going_down = lax.ppermute(going_down, axis, [(d, (d - 1) % ways) for d in range(ways)])
+            full = lax.dynamic_update_slice_in_dim(
+                full, going_down, (here + far) % ways * step, axis=dim
+            )
+    return full
 
 
 def extended(block, sides, width):
@@ -49,7 +67,7 @@
     quarter = lax.dynamic_slice_in_dim(whole_rows, share * piece, piece, 2)
     for repeat in range(STEPS):
         halo_part = extended(quarter, (("grid", 0),), reach)
-        halo_rows = lax.all_gather(halo_part, "layer", axis=2, tiled=True)
+        halo_rows = gather_around(halo_part, "layer", 2)
         square = jnp.where(kept, strip_product(quarter, halo_rows, reach), 0.0).astype(jnp.bfloat16)
         cube = jnp.where(kept, strip_product(square, halo_rows, reach), 0.0)
         quarter = (

time: 161 us -> 195 us (1.21)
  local copies, waits for them, and re-layouts: 4.62 us -> 28.5 us
  matrix products: 23.9 us -> 40.6 us
  between operations: 13.6 us -> 0.23 us
  waiting for transfers between devices: 104 us -> 108 us
  starting transfers between devices: 11 us -> 14.5 us
    ppermute x0 -> x6, waiting for transfers between devices: none -> 85 us  [the longest x4 85 us: gather_around(): lax.ppermute(going_up, axis, [(d, (d + 1) % ways) for d in range(ways)])]
    all_gather x2 -> x0, waiting for transfers between devices: 80.6 us -> none  [per_device(): halo_rows = lax.all_gather(halo_part, 'layer', axis=2, tiled=True)]
    slice x0 -> x2, local copies, waits for them, and re-layouts: none -> 17.2 us  [strip_product(): padded[offset:offset + row_count, 2 * reach - offset:2 * reach - offset +...]
    dot_general x36, matrix products: 23.9 us -> 40.6 us  [strip_product(): jnp.einsum('rab,rwbc->rwac', left_rows[:, offset], source, preferred_elem...]
    dynamic_update_slice x0 -> x6, local copies, waits for them, and re-layouts: none -> 5.95 us  [the longest x4 3.96 us: gather_around(): lax.dynamic_update_slice_in_dim(full, going_up, (here - far) % ways * ste...]
    ppermute x0 -> x6, starting transfers between devices: none -> 3.62 us  [the longest x2 3.48 us: gather_around(): lax.ppermute(going_down, axis, [(d, (d - 1) % ways) for d in range(ways)])]
    another operation x0 -> x2, local copies, waits for them, and re-layouts: none -> 2.64 us
  transfers between devices with their start and end apart: 6 -> 10, of which waited for: 6 -> 8; matrix products, arithmetic and copies ran while one was open for 0% -> 4% of each run, Pallas kernels for 0% -> 0%
where the time goes in v1:
time: 195 us
  waiting for transfers between devices  108 us (55%)
  matrix products  40.6 us (21%)
  local copies, waits for them, and re-layouts  28.5 us (15%)
  starting transfers between devices  14.5 us (7%)
  other arithmetic  3.11 us (2%)
    ppermute x4, waiting for transfers between devices, gather_around(): lax.ppermute(going_up, axis, [(d, (d + 1) % ways) for d in range(ways)])  85 us
    dot_general x36, matrix products, strip_product(): jnp.einsum('rab,rwbc->rwac', left_rows[:, offset], source, preferred_elem...  40.6 us
    ppermute x2, waiting for transfers between devices, extended(): lax.ppermute(lax.slice_in_dim(block, block.shape[dim] - width, None, axis...  17.9 us
    slice x2, local copies, waits for them, and re-layouts, strip_product(): padded[offset:offset + row_count, 2 * reach - offset:2 * reach - offset +...  17.2 us
    ppermute x2, starting transfers between devices, extended(): lax.ppermute(lax.slice_in_dim(block, 0, width, axis=dim), axis, backward)  7.55 us
    ppermute x2, waiting for transfers between devices, extended(): lax.ppermute(lax.slice_in_dim(block, 0, width, axis=dim), axis, backward)  5.07 us
    dynamic_update_slice x4, local copies, waits for them, and re-layouts, gather_around(): lax.dynamic_update_slice_in_dim(full, going_up, (here - far) % ways * ste...  3.96 us
  transfers between devices with their start and end apart: 10, of which 8 were waited for; matrix products, arithmetic and copies ran while one was open for 4% of the time, Pallas kernels for 0%

profile of v1, /device:TPU:0, one launch (start us, length us, event | category | flops | bytes accessed | tf_op | source)
XLA Modules:
  0.0 194.9 jit_solution(9540432226506608698)
XLA Ops:
  0.0 0.9 broadcast_compare_fusion
  1.0 0.9 copy-done
  2.1 3.0 %collective-permute-start = (bf16[4,9,32,128]{3,2,0,1:T(8,128)(2,1)S(1)}, bf16[4,9,32,128]{3,2,0,1:T(8,128)(2,1)S(1)}, u32[]{:S(2)}, u32[]{:S(2)}) collective-permute-start(bf16[4,9,32,128]{3,2,0,1:T(8,128)(2,1)S(1)} %get-tuple-element.25), channel_id=1, source_target_pairs={{0,1},{1,2},{2,3},{3,4},{4,5},{5,6},{6,7},{7,0},{8,9},{9,10},{10,1... | collective-permute-start | bytes 884744 | tf_op jit(solution)/shard_map/ppermute | solution.py:33
  5.2 3.1 %collective-permute-start.1 = (bf16[4,9,32,128]{3,2,0,1:T(8,128)(2,1)S(1)}, bf16[4,9,32,128]{3,2,0,1:T(8,128)(2,1)S(1)}, u32[]{:S(2)}, u32[]{:S(2)}) collective-permute-start(bf16[4,9,32,128]{3,2,0,1:T(8,128)(2,1)S(1)} %get-tuple-element.26), channel_id=1, source_target_pairs={{1,0},{2,1},{3,2},{4,3},{5,4},{6,5},{7,6},{0,7},{9,8},{10,9},{11,1... | collective-permute-start | bytes 884744 | tf_op jit(solution)/shard_map/ppermute | solution.py:36
  8.3 9.5 %collective-permute-done = bf16[4,9,32,128]{3,2,0,1:T(8,128)(2,1)S(1)} collective-permute-done((bf16[4,9,32,128]{3,2,0,1:T(8,128)(2,1)S(1)}, bf16[4,9,32,128]{3,2,0,1:T(8,128)(2,1)S(1)}, u32[]{:S(2)}, u32[]{:S(2)}) %collective-permute-start) | collective-permute-done | bytes 294944 | tf_op jit(solution)/shard_map/ppermute | solution.py:33
  17.8 2.2 %collective-permute-done.1 = bf16[4,9,32,128]{3,2,0,1:T(8,128)(2,1)S(1)} collective-permute-done((bf16[4,9,32,128]{3,2,0,1:T(8,128)(2,1)S(1)}, bf16[4,9,32,128]{3,2,0,1:T(8,128)(2,1)S(1)}, u32[]{:S(2)}, u32[]{:S(2)}) %collective-permute-start.1) | collective-permute-done | bytes 294944 | tf_op jit(solution)/shard_map/ppermute | solution.py:36
  20.0 1.2 pad_maximum_fusion
  21.2 1.7 collective-permute-start.3
  22.9 28.2 %collective-permute-done.2 = bf16[18,9,32,128]{3,2,0,1:T(8,128)(2,1)} collective-permute-done((bf16[18,9,32,128]{3,2,0,1:T(8,128)(2,1)}, bf16[18,9,32,128]{3,2,0,1:T(8,128)(2,1)}, u32[]{:S(2)}, u32[]{:S(2)}) %collective-permute-start.2) | collective-permute-done | bytes 1327136 | tf_op jit(solution)/shard_map/ppermute | solution.py:17
  51.2 1.3 broadcast.23.clone
  52.6 0.3 copy_dynamic-update-slice_fusion.7
  52.9 1.7 copy_dynamic-update-slice_fusion.6
  54.6 1.7 copy_dynamic-update-slice_fusion.5
  56.3 12.4 %collective-permute-done.4 = bf16[18,9,32,128]{3,2,0,1:T(8,128)(2,1)} collective-permute-done((bf16[18,9,32,128]{3,2,0,1:T(8,128)(2,1)}, bf16[18,9,32,128]{3,2,0,1:T(8,128)(2,1)}, u32[]{:S(2)}, u32[]{:S(2)}) %collective-permute-start.4) | collective-permute-done | bytes 1327136 | tf_op jit(solution)/shard_map/ppermute | solution.py:17
  68.7 1.6 copy_dynamic-update-slice_fusion.4
  70.3 9.0 %pad_slice_fusion.14 = (bf16[10,9,128,128]{3,2,1,0:T(8,128)(2,1)}, bf16[10,9,128,128]{3,2,1,0:T(8,128)(2,1)S(1)}, bf16[10,9,128,128]{3,2,1,0:T(8,128)(2,1)S(1)},...) fusion(bf16[18,9,128,128]{3,2,1,0:T(8,128)(2,1)S(1)} %copy_dyna, ...), kind=kLoop, calls=%fused_computation.14 | loop fusion | bytes 34799616 | tf_op jit(solution)/shard_map/slice | solution.py:49
  79.4 0.6 fusion.44
  79.9 0.6 fusion.48
  80.5 0.6 fusion.52
  81.1 0.6 fusion.56
  81.6 1.7 fusion.60
  83.3 0.7 copy-done.3
  84.0 1.7 fusion.64
  85.7 1.7 fusion.68
  87.4 1.7 fusion.40
  89.1 4.7 %fusion.84 = bf16[10,9,32,128]{3,2,0,1:T(8,128)(2,1)} fusion(bf16[10,9,128,128]{3,2,1,0:T(8,128)(2,1)S(1)} %get-tuple-element.20, f32[10,9,128,32]{2,3,0,1:T(8,128)} %fusion.40, f32[10,9,128,32]{2,3,0,1:T(8,128)S(1)} %fusion.44, f32[10,9,128,32]{2,3,0,1:T(8,128)S(1)} %fusion.48, f32[10,9,128,32]{2,3,0,1:T(8,128)S(1)} %fusion.52, ...), kind=kOutput, calls=%fused_computation.106 | convolution fusion | flops 98058240 | bytes 15566848 | tf_op jit(solution)/shard_map/rab,rwbc->rwac/dot_general | solution.py:52
  93.8 1.5 fusion.66
  95.4 0.6 fusion.70
  95.9 0.6 fusion.62
  96.5 0.6 fusion.58
  97.0 0.6 fusion.54
  97.6 0.6 fusion.50
  98.2 0.6 fusion.46
  98.7 0.6 fusion.42
  99.3 2.1 %fusion.75 = bf16[10,9,32,128]{3,2,0,1:T(8,128)(2,1)S(1)} fusion(f32[10,9,128,32]{2,3,0,1:T(8,128)S(1)} %fusion.42, f32[10,9,128,32]{2,3,0,1:T(8,128)S(1)} %fusion.46, f32[10,9,128,32]{2,3,0,1:T(8,128)S(1)} %fusion.50, f32[10,9,128,32]{2,3,0,1:T(8,128)S(1)} %fusion.54, f32[10,9,128,32]{2,3,0,1:T(8,128)S(1)} %fusion.58, f32[10,9,128,32]{2,3,0,1:T(8,128)S(1)} %fusion.62, ...), kind=kOutput, calls=%fused_computation.93 | convolution fusion | flops 100270080 | bytes 16306180 | tf_op jit(solution)/shard_map/rab,rwbc->rwac/dot_general | solution.py:52
  101.5 0.3 collective-permute-start.5
  101.8 4.4 %collective-permute-start.6 = (bf16[4,9,32,128]{3,2,0,1:T(8,128)(2,1)S(1)}, bf16[4,9,32,128]{3,2,0,1:T(8,128)(2,1)S(1)}, u32[]{:S(2)}, u32[]{:S(2)}) collective-permute-start(bf16[4,9,32,128]{3,2,0,1:T(8,128)(2,1)S(1)} %get-tuple-element.24), channel_id=1, source_target_pairs={{1,0},{2,1},{3,2},{4,3},{5,4},{6,5},{7,6},{0,7},{9,8},{10,9},{11,1... | collective-permute-start | bytes 884744 | tf_op jit(solution)/shard_map/ppermute | solution.py:36
  106.3 8.4 %collective-permute-done.5 = bf16[4,9,32,128]{3,2,0,1:T(8,128)(2,1)S(1)} collective-permute-done((bf16[4,9,32,128]{3,2,0,1:T(8,128)(2,1)S(1)}, bf16[4,9,32,128]{3,2,0,1:T(8,128)(2,1)S(1)}, u32[]{:S(2)}, u32[]{:S(2)}) %collective-permute-start.5) | collective-permute-done | bytes 294944 | tf_op jit(solution)/shard_map/ppermute | solution.py:33
  114.7 2.9 %collective-permute-done.6 = bf16[4,9,32,128]{3,2,0,1:T(8,128)(2,1)S(1)} collective-permute-done((bf16[4,9,32,128]{3,2,0,1:T(8,128)(2,1)S(1)}, bf16[4,9,32,128]{3,2,0,1:T(8,128)(2,1)S(1)}, u32[]{:S(2)}, u32[]{:S(2)}) %collective-permute-start.6) | collective-permute-done | bytes 294944 | tf_op jit(solution)/shard_map/ppermute | solution.py:36
  117.7 1.7 collective-permute-start.8
  119.5 29.6 %collective-permute-done.7 = bf16[18,9,32,128]{3,2,0,1:T(8,128)(2,1)S(1)} collective-permute-done((bf16[18,9,32,128]{3,2,0,1:T(8,128)(2,1)S(1)}, bf16[18,9,32,128]{3,2,0,1:T(8,128)(2,1)S(1)}, u32[]{:S(2)}, u32[]{:S(2)}) %collective-permute-start.7) | collective-permute-done | bytes 1327136 | tf_op jit(solution)/shard_map/ppermute | solution.py:17
  149.0 1.3 broadcast.23
  150.4 0.3 copy_dynamic-update-slice_fusion.3
  151.4 14.8 %collective-permute-done.9 = bf16[18,9,32,128]{3,2,0,1:T(8,128)(2,1)S(1)} collective-permute-done((bf16[18,9,32,128]{3,2,0,1:T(8,128)(2,1)S(1)}, bf16[18,9,32,128]{3,2,0,1:T(8,128)(2,1)S(1)}, u32[]{:S(2)}, u32[]{:S(2)}) %collective-permute-start.9) | collective-permute-done | bytes 1327136 | tf_op jit(solution)/shard_map/ppermute | solution.py:17
  166.6 8.2 %pad_slice_fusion.6 = (bf16[10,9,128,128]{3,2,1,0:T(8,128)(2,1)}, bf16[10,9,128,128]{3,2,1,0:T(8,128)(2,1)S(1)}, bf16[10,9,128,128]{3,2,1,0:T(8,128)(2,1)S(1)}, ...) fusion(bf16[18,9,128,128]{3,2,1,0:T(8,128)(2,1)S(1)} %copy_dyna, ...), kind=kLoop, calls=%fused_computation.6 | loop fusion | bytes 34799616 | tf_op jit(solution)/shard_map/slice | solution.py:49
  174.7 2.4 %fusion.28 = f32[10,9,128,32]{2,3,0,1:T(8,128)S(1)} fusion(bf16[10,9,128,128]{3,2,1,0:T(8,128)(2,1)} %get-tuple-element.5, bf16[10,9,32,128]{3,2,0,1:T(8,128)(2,1)S(1)} %fusion.75), kind=kOutput, calls=%fused_computation.44 | convolution fusion | flops 94371840 | bytes 4505600 | tf_op jit(solution)/shard_map/rab,rwbc->rwac/dot_general | solution.py:52
  177.1 0.6 fusion.32
  177.7 0.6 fusion.24
  178.3 0.6 fusion.20
  178.8 0.6 fusion.16
  179.4 0.6 fusion.12
  179.9 1.7 fusion.8
  181.7 1.7 fusion.4
  183.3 4.0 %fusion.87 = bf16[10,9,32,128]{3,2,0,1:T(8,128)(2,1)} fusion(bf16[10,9,128,128]{3,2,1,0:T(8,128)(2,1)S(1)} %get-tuple-element.11, f32[10,9,128,32]{2,3,0,1:T(8,128)} %fusion.4, f32[10,9,128,32]{2,3,0,1:T(8,128)} %fusion.8, f32[10,9,128,32]{2,3,0,1:T(8,128)S(1)} %fusion.12, f32[10,9,128,32]{2,3,0,1:T(8,128)S(1)} %fusion.16, ...), kind=kOutput, calls=%fused_computation.107 | convolution fusion | flops 98058240 | bytes 15566848 | tf_op jit(solution)/shard_map/rab,rwbc->rwac/dot_general | solution.py:52
  187.3 1.5 fusion.30
  188.9 0.6 fusion.34
  189.4 0.6 fusion.26
  190.0 0.6 fusion.22
  190.5 0.6 fusion.18
  191.1 0.6 fusion.14
  191.7 0.6 fusion.10
  192.2 0.6 fusion.6
  192.8 1.2 fusion.73
  194.0 0.9 copy.50
  (30 shorter events, 1.7 us)
Async XLA Ops:
  0.0 1.8 copy-start
  2.1 17.9 %copy-start.5 = (bf16[10,9,32,128]{3,2,0,1:T(8,128)(2,1)}, bf16[10,9,32,128]{3,2,0,1:T(8,128)(2,1)S(1)}, u32[]{:S(2)}) copy-start(bf16[10,9,32,128]{3,2,0,1:T(8,128)(2,1)S(1)} %copy_select_fusion) | copy-start | bytes 2211844
  2.1 15.6 %collective-permute-start = (bf16[4,9,32,128]{3,2,0,1:T(8,128)(2,1)S(1)}, bf16[4,9,32,128]{3,2,0,1:T(8,128)(2,1)S(1)}, u32[]{:S(2)}, u32[]{:S(2)}) collective-permute-start(bf16[4,9,32,128]{3,2,0,1:T(8,128)(2,1)S(1)} %get-tuple-element.25), channel_id=1, source_target_pairs={{0,1},{1,2},{2,3},{3,4},{4,5},{5,6},{6,7},{7,0},{8,9},{9,10},{10,1... | collective-permute-start | bytes 884744 | tf_op jit(solution)/shard_map/ppermute | solution.py:33
  5.2 14.8 %collective-permute-start.1 = (bf16[4,9,32,128]{3,2,0,1:T(8,128)(2,1)S(1)}, bf16[4,9,32,128]{3,2,0,1:T(8,128)(2,1)S(1)}, u32[]{:S(2)}, u32[]{:S(2)}) collective-permute-start(bf16[4,9,32,128]{3,2,0,1:T(8,128)(2,1)S(1)} %get-tuple-element.26), channel_id=1, source_target_pairs={{1,0},{2,1},{3,2},{4,3},{5,4},{6,5},{7,6},{0,7},{9,8},{10,9},{11,1... | collective-permute-start | bytes 884744 | tf_op jit(solution)/shard_map/ppermute | solution.py:36
  21.2 30.0 %collective-permute-start.2 = (bf16[18,9,32,128]{3,2,0,1:T(8,128)(2,1)}, bf16[18,9,32,128]{3,2,0,1:T(8,128)(2,1)}, u32[]{:S(2)}, u32[]{:S(2)}) collective-permute-start(bf16[18,9,32,128]{3,2,0,1:T(8,128)(2,1)} %pad_maximum_fusion), channel_id=1, source_target_pairs={{0,8},{8,16},{16,24},{24,0},{1,9},{9,17},{17,25},{25,1},{2,10},{10... | collective-permute-start | bytes 3981320 | tf_op jit(solution)/shard_map/ppermute | solution.py:17
  21.2 33.4 %collective-permute-start.3 = (bf16[18,9,32,128]{3,2,0,1:T(8,128)(2,1)}, bf16[18,9,32,128]{3,2,0,1:T(8,128)(2,1)}, u32[]{:S(2)}, u32[]{:S(2)}) collective-permute-start(bf16[18,9,32,128]{3,2,0,1:T(8,128)(2,1)} %pad_maximum_fusion), channel_id=1, source_target_pairs={{0,24},{8,0},{16,8},{24,16},{1,25},{9,1},{17,9},{25,17},{2,26},{10... | collective-permute-start | bytes 3981320 | tf_op jit(solution)/shard_map/ppermute | solution.py:20
  51.2 17.5 %collective-permute-start.4 = (bf16[18,9,32,128]{3,2,0,1:T(8,128)(2,1)}, bf16[18,9,32,128]{3,2,0,1:T(8,128)(2,1)}, u32[]{:S(2)}, u32[]{:S(2)}) collective-permute-start(bf16[18,9,32,128]{3,2,0,1:T(8,128)(2,1)} %collective-permute-done.2), channel_id=1, source_target_pairs={{0,8},{8,16},{16,24},{24,0},{1,9},{9,17},{17,25},{25,1},{2,10},{10... | collective-permute-start | bytes 3981320 | tf_op jit(solution)/shard_map/ppermute | solution.py:17
  51.2 1.3 copy-start.6
  81.6 2.4 %copy-start.3 = (bf16[10,9,128,128]{3,2,1,0:T(8,128)(2,1)S(1)}, bf16[10,9,128,128]{3,2,1,0:T(8,128)(2,1)}, u32[]{:S(2)}) copy-start(bf16[10,9,128,128]{3,2,1,0:T(8,128)(2,1)} %get-tuple-element.14) | copy-start | bytes 8847364
  83.3 2.4 %copy-start.2 = (bf16[10,9,128,128]{3,2,1,0:T(8,128)(2,1)S(1)}, bf16[10,9,128,128]{3,2,1,0:T(8,128)(2,1)}, u32[]{:S(2)}) copy-start(bf16[10,9,128,128]{3,2,1,0:T(8,128)(2,1)} %get-tuple-element.22) | copy-start | bytes 8847364
  93.8 1.5 copy-start.8
  101.5 13.2 %collective-permute-start.5 = (bf16[4,9,32,128]{3,2,0,1:T(8,128)(2,1)S(1)}, bf16[4,9,32,128]{3,2,0,1:T(8,128)(2,1)S(1)}, u32[]{:S(2)}, u32[]{:S(2)}) collective-permute-start(bf16[4,9,32,128]{3,2,0,1:T(8,128)(2,1)S(1)} %get-tuple-element.23), channel_id=1, source_target_pairs={{0,1},{1,2},{2,3},{3,4},{4,5},{5,6},{6,7},{7,0},{8,9},{9,10},{10,1... | collective-permute-start | bytes 884744 | tf_op jit(solution)/shard_map/ppermute | solution.py:33
  101.8 15.7 %collective-permute-start.6 = (bf16[4,9,32,128]{3,2,0,1:T(8,128)(2,1)S(1)}, bf16[4,9,32,128]{3,2,0,1:T(8,128)(2,1)S(1)}, u32[]{:S(2)}, u32[]{:S(2)}) collective-permute-start(bf16[4,9,32,128]{3,2,0,1:T(8,128)(2,1)S(1)} %get-tuple-element.24), channel_id=1, source_target_pairs={{1,0},{2,1},{3,2},{4,3},{5,4},{6,5},{7,6},{0,7},{9,8},{10,9},{11,1... | collective-permute-start | bytes 884744 | tf_op jit(solution)/shard_map/ppermute | solution.py:36
  117.7 31.4 %collective-permute-start.7 = (bf16[18,9,32,128]{3,2,0,1:T(8,128)(2,1)S(1)}, bf16[18,9,32,128]{3,2,0,1:T(8,128)(2,1)S(1)}, u32[]{:S(2)}, u32[]{:S(2)}) collective-permute-start(bf16[18,9,32,128]{3,2,0,1:T(8,128)(2,1)S(1)} %pad_maximum_fusion.1), channel_id=1, source_target_pairs={{0,8},{8,16},{16,24},{24,0},{1,9},{9,17},{17,25},{25,1},{2,10},{10... | collective-permute-start | bytes 3981320 | tf_op jit(solution)/shard_map/ppermute | solution.py:17
  117.7 33.3 %collective-permute-start.8 = (bf16[18,9,32,128]{3,2,0,1:T(8,128)(2,1)S(1)}, bf16[18,9,32,128]{3,2,0,1:T(8,128)(2,1)S(1)}, u32[]{:S(2)}, u32[]{:S(2)}) collective-permute-start(bf16[18,9,32,128]{3,2,0,1:T(8,128)(2,1)S(1)} %pad_maximum_fusion.1), channel_id=1, source_target_pairs={{0,24},{8,0},{16,8},{24,16},{1,25},{9,1},{17,9},{25,17},{2,26},{10... | collective-permute-start | bytes 3981320 | tf_op jit(solution)/shard_map/ppermute | solution.py:20
  149.0 17.2 %collective-permute-start.9 = (bf16[18,9,32,128]{3,2,0,1:T(8,128)(2,1)S(1)}, bf16[18,9,32,128]{3,2,0,1:T(8,128)(2,1)S(1)}, u32[]{:S(2)}, u32[]{:S(2)}) collective-permute-start(bf16[18,9,32,128]{3,2,0,1:T(8,128)(2,1)S(1)} %collective-permute-done.7), channel_id=1, source_target_pairs={{0,8},{8,16},{16,24},{24,0},{1,9},{9,17},{17,25},{25,1},{2,10},{10... | collective-permute-start | bytes 3981320 | tf_op jit(solution)/shard_map/ppermute | solution.py:17
  183.3 4.0 %copy-start.4 = (bf16[10,9,128,128]{3,2,1,0:T(8,128)(2,1)S(1)}, bf16[10,9,128,128]{3,2,1,0:T(8,128)(2,1)}, u32[]{:S(2)}) copy-start(bf16[10,9,128,128]{3,2,1,0:T(8,128)(2,1)} %get-tuple-element.5) | copy-start | bytes 8847364
  187.3 1.5 copy-start.7
  192.8 2.1 %copy-start.1 = (bf16[10,9,128,128]{3,2,1,0:T(8,128)(2,1)S(1)}, bf16[10,9,128,128]{3,2,1,0:T(8,128)(2,1)}, u32[]{:S(2)}) copy-start(bf16[10,9,128,128]{3,2,1,0:T(8,128)(2,1)} %param.2) | copy-start | bytes 8847364
